TPU v7x, 256 devices: a whole 4x4x8 slice. The times are simulated.
256 devices in a mesh: dp: 16 (over z_hi, y), sub: 16 (over x, z_lo, core).
Axes of the slice: x: 4, y: 4, z: 8 (z_hi: 4, z_lo: 2; z = z_hi * 2 + z_lo), core: 2. Of those that a mesh axis runs over, the one named last changes fastest.
Arguments:
- vectors: bfloat16 [32768, 2048], P(('dp', 'sub')), may hold values from -24 to 24
- rotation: bfloat16 [2048, 2048], P(None, 'sub'), may hold values from -0.125 to 0.125
- codebook: bfloat16 [16, 4096, 128], P('sub'), may hold values from -6 to 6
- codes: int32 [32768, 16], P('dp', 'sub'), may hold values from 0 to 4095
Outputs:
- centroids: bfloat16 [16, 4096, 128], P('sub')
- distortion: float32 [32768, 16], P('dp', 'sub')
- cross: float32 [2048, 2048], P('dp', 'sub')
All inputs are finite; a program needn't handle non-finite values.
Results may differ from a plain program's by a relative error of at most 0.0047.
Values may be sent and summed in bfloat16 or wider, within the bound.
A program may use at most 64 MiB of HBM per device.

v0:
```python
import jax
import jax.numpy as jnp
from jax import lax
from jax.sharding import PartitionSpec as P


def class_sums(values, labels, count):
    totals = jax.ops.segment_sum(values.astype(jnp.float32), labels, num_segments=count)
    members = jax.ops.segment_sum(jnp.ones(labels.shape, jnp.float32), labels, num_segments=count)
    return (totals, members)


def update_rule(totals, members, codewords):
    return ((totals + codewords.astype(jnp.float32)) / (members[..., None] + 1.0)).astype(
        jnp.bfloat16
    )


def per_device(vectors, rotation, codebook, codes):
    local_sub = codebook.shape[0]
    count = codebook.shape[1]
    sub_width = codebook.shape[2]
    rotated = jnp.dot(
        vectors,
        lax.all_gather(rotation, "sub", axis=1, tiled=True),
        preferred_element_type=jnp.float32,
    ).astype(jnp.bfloat16)
    grouped = lax.all_to_all(rotated, "sub", split_axis=1, concat_axis=0, tiled=True)
    group_rows = grouped.shape[0]
    values = grouped.reshape(group_rows, local_sub, sub_width).transpose(1, 0, 2)
    labels = codes.T
    totals, members = jax.vmap(class_sums, in_axes=(0, 0, None))(values, labels, count)
    totals, members = lax.psum((totals, members), "dp")
    centroid = update_rule(totals, members, codebook)
    rebuilt = jax.vmap(lambda table, index: jnp.take(table, index, axis=0))(centroid, labels)
    distance = jnp.sum((values.astype(jnp.float32) - rebuilt.astype(jnp.float32)) ** 2, axis=-1)
    rebuilt_flat = rebuilt.transpose(1, 0, 2).reshape(group_rows, local_sub * sub_width)
    gathered = lax.all_gather(vectors, "sub", axis=0, tiled=True)
    product = lax.dot_general(
        gathered, rebuilt_flat, (((0,), (0,)), ((), ())), preferred_element_type=jnp.float32
    )
    cross = lax.psum_scatter(product, "dp", scatter_dimension=0, tiled=True)
    return (centroid, distance.T, cross)


def solution(mesh):
    placed = (P(("dp", "sub"), None), P(None, "sub"), P("sub", None, None), P("dp", "sub"))
    return jax.shard_map(
        per_device,
        mesh=mesh,
        in_specs=placed,
        out_specs=(P("sub", None, None), P("dp", "sub"), P("dp", "sub")),
        check_vma=False,
    )
```

profile of v0, /device:TPU:2, one launch (start us, length us, event | category | flops | bytes accessed | tf_op | source)
XLA Modules:
  0.0 444.4 jit_solution(17929500264021960550)
XLA Ops:
  7.2 0.0 all-gather.3.cloned.1.call-start
  7.2 0.7 all-gather.3.cloned.1.call-update
  7.9 68.8 %all-gather.3.cloned.1.call-done = bf16[2048,2048]{1,0:T(8,128)(2,1)} async-done(((bf16[2048,128]{1,0:T(8,128)(2,1)}), bf16[2048,2048]{1,0:T(8,128)(2,1)}) %all-gather.3.cloned.1.call-update) | async-done | bytes 8388624 | tf_op jit(solution)/shard_map/all_gather | solution.py:25
  76.7 4.8 %fusion = bf16[16,16,8,128]{3,2,1,0:T(8,128)(2,1)S(1)} fusion(bf16[128,2048]{1,0:T(8,128)(2,1)} %param.4, bf16[2048,2048]{1,0:T(8,128)(2,1)} %all-gather.3.cloned.1.call-done), kind=kOutput, calls=%fused_computation.6 | convolution fusion | flops 1074003968 | bytes 9437184 | tf_op jit(solution)/shard_map/dot_general | solution.py:23
  81.5 0.0 copy-start.2
  81.5 0.0 copy-start.3
  81.6 0.0 copy-start.4
  81.6 0.9 copy.25
  82.5 4.5 %all-to-all-start = ((bf16[128,16,128]{2,0,1:T(8,128)(2,1)}), bf16[128,16,128]{2,0,1:T(8,128)(2,1)S(1)}, u32[]{:S(2)}, u32[]{:S(2)}) async-start(bf16[128,16,128]{2,0,1:T(8,128)(2,1)} %bitcast.29), calls=%async_computation | async-start | bytes 1048576 | tf_op jit(solution)/shard_map/all_to_all | solution.py:28
  87.0 0.0 all-reduce.2.cloned.1.call-start
  87.1 0.1 fusion.8
  87.2 0.1 and_reduce_fusion
  87.3 8.0 %all-to-all-done = bf16[128,16,128]{2,0,1:T(8,128)(2,1)S(1)} async-done(((bf16[128,16,128]{2,0,1:T(8,128)(2,1)}), bf16[128,16,128]{2,0,1:T(8,128)(2,1)S(1)}, u32[]{:S(2)}, u32[]{:S(2)}) %all-to-all-start) | async-done | bytes 524320 | tf_op jit(solution)/shard_map/all_to_all | solution.py:28
  95.3 0.1 convert_element_type.48
  95.4 0.0 copy-start.1
  95.4 12.8 %scatter_custom_fusion = f32[4096,128]{1,0:T(8,128)} fusion(s32[2048]{0:T(1024)S(1)} %broadcast_select_fusion, f32[2048,128]{1,0:T(8,128)S(1)} %bitcast.33, f32[]{:T(128)} %constant.6.clone.1), kind=kCustom, calls=%fused_computation.10 | custom fusion | flops 262144 | bytes 2097156
  108.3 0.0 all-reduce.2.cloned.1.call-update
  108.3 0.0 all-gather.5.cloned.1.call-start
  108.3 0.7 all-gather.5.cloned.1.call-update
  109.0 0.0 reduce-scatter.2.cloned.1.call-start
  109.1 11.2 %scatter_custom_fusion.1 = f32[4096]{0:T(1024)S(1)} fusion(s32[2048]{0:T(1024)S(1)} %broadcast_select_fusion, f32[2048]{0:T(1024)S(1)} %broadcast.100, f32[]{:T(128)} %constant.6.clone.1), kind=kCustom, calls=%fused_computation.28 | custom fusion | flops 2048 | bytes 16388
  120.3 82.3 %psum.15 = f32[1,4096]{1,0:T(1,128)S(1)} all-reduce(f32[1,4096]{1,0:T(1,128)S(1)} %bitcast.39), channel_id=1, replica_groups=mesh['dp'=16,'sub'=16] {'dp'}, use_global_device_ids=true, to_apply=%region_3.0 | all-reduce | flops 4096 | bytes 32768 | tf_op jit(solution)/shard_map/psum | solution.py:33
  202.8 84.2 %all-reduce.2.cloned.1.call-done = f32[1,4096,128]{2,1,0:T(8,128)} async-done(((f32[1,4096,128]{2,1,0:T(8,128)}), f32[1,4096,128]{2,1,0:T(8,128)}) %all-reduce.2.cloned.1.call-update) | async-done | bytes 2097168 | tf_op jit(solution)/shard_map/psum | solution.py:33
  287.0 2.0 divide_convert_fusion
  289.0 0.0 copy-start
  289.0 8.6 %gather_fusion = bf16[2048,128]{1,0:T(8,128)(2,1)S(1)} fusion(bf16[1,4096,128]{2,1,0:T(8,128)(2,1)S(1)} %divide_convert_fusion, s32[2048]{0:T(1024)S(1)} %bitcast.30), kind=kCustom, calls=%fused_computation | custom fusion | bytes 1064960 | tf_op jit(solution)/shard_map/vmap(jit(_take))/gather | solution.py:35
  297.6 45.2 %all-gather.5.cloned.1.call-done = bf16[2048,2048]{1,0:T(8,128)(2,1)} async-done(((bf16[128,2048]{1,0:T(8,128)(2,1)}), bf16[2048,2048]{1,0:T(8,128)(2,1)}) %all-gather.5.cloned.1.call-update) | async-done | bytes 8388624 | tf_op jit(solution)/shard_map/all_gather | solution.py:38
  342.7 5.9 %convolution_bitcast_fusion = f32[2048,128]{0,1:T(8,128)} fusion(bf16[2048,2048]{1,0:T(8,128)(2,1)} %all-gather.5.cloned.1.call-done, bf16[2048,128]{1,0:T(8,128)(2,1)S(1)} %gather_fusion, pred[2048]{0:T(1024)(128)(4,1)S(1)} %compare_and_fusion), kind=kOutput, calls=%fused_computation.3 | convolution fusion | flops 1074003968 | bytes 9963520 | tf_op jit(solution)/shard_map/dot_general | solution.py:39
  348.6 0.0 reduce-scatter.2.cloned.1.call-update
  348.6 1.2 fusion.2
  349.9 86.4 %reduce-scatter.2.cloned.1.call-done = f32[128,128]{0,1:T(8,128)} async-done(((f32[2048,128]{0,1:T(8,128)}), f32[128,128]{0,1:T(8,128)}) %reduce-scatter.2.cloned.1.call-update) | async-done | bytes 65552 | tf_op jit(solution)/shard_map/reduce_scatter | solution.py:42
  436.3 1.6 copy.21
  (13 shorter events, 0.1 us)
Async XLA Ops:
  7.2 69.5 %all-gather.3.cloned.1.call-start = ((), (), s32[]{:S(2)}) async-start(), calls=%async_computation.2 | async-start | bytes 8912896 | tf_op jit(solution)/shard_map/all_gather | solution.py:25
  81.5 5.5 %copy-start.2 = (s32[2048,1]{0,1:T(1,128)S(1)}, s32[2048,1]{0,1:T(1,128)}, u32[]{:S(2)}) copy-start(s32[2048,1]{0,1:T(1,128)} %param.7) | copy-start | bytes 24580
  81.5 5.5 %copy-start.3 = (s32[2]{0:T(128)S(1)}, s32[2]{0:T(128)}, u32[]{:S(2)}) copy-start(s32[2]{0:T(128)} %constant.26) | copy-start | bytes 28
  81.6 5.6 %copy-start.4 = (s32[2]{0:T(128)S(1)}, s32[2]{0:T(128)}, u32[]{:S(2)}) copy-start(s32[2]{0:T(128)} %constant.29) | copy-start | bytes 28
  82.5 12.8 %all-to-all-start = ((bf16[128,16,128]{2,0,1:T(8,128)(2,1)}), bf16[128,16,128]{2,0,1:T(8,128)(2,1)S(1)}, u32[]{:S(2)}, u32[]{:S(2)}) async-start(bf16[128,16,128]{2,0,1:T(8,128)(2,1)} %bitcast.29), calls=%async_computation | async-start | bytes 1048576 | tf_op jit(solution)/shard_map/all_to_all | solution.py:28
  87.0 199.9 %all-reduce.2.cloned.1.call-start = ((), (), s32[]{:S(2)}) async-start(), calls=%async_computation.3 | async-start | bytes 4194304 | tf_op jit(solution)/shard_map/psum | solution.py:33
  95.4 191.6 %copy-start.1 = (bf16[1,4096,128]{2,1,0:T(8,128)(2,1)S(1)}, bf16[1,4096,128]{2,1,0:T(8,128)(2,1)}, u32[]{:S(2)}) copy-start(bf16[1,4096,128]{2,1,0:T(8,128)(2,1)} %param.6) | copy-start | bytes 3145732
  108.3 234.5 %all-gather.5.cloned.1.call-start = ((), (), s32[]{:S(2)}) async-start(), calls=%async_computation.4 | async-start | bytes 8912896 | tf_op jit(solution)/shard_map/all_gather | solution.py:38
  109.0 327.3 %reduce-scatter.2.cloned.1.call-start = ((), (), s32[]{:S(2)}) async-start(), calls=%async_computation.5 | async-start | bytes 1114112 | tf_op jit(solution)/shard_map/reduce_scatter | solution.py:42
  289.0 8.6 %copy-start = (bf16[1,4096,128]{2,1,0:T(8,128)(2,1)}, bf16[1,4096,128]{2,1,0:T(8,128)(2,1)S(1)}, u32[]{:S(2)}) copy-start(bf16[1,4096,128]{2,1,0:T(8,128)(2,1)S(1)} %divide_convert_fusion) | copy-start | bytes 3145732
Sparse Core Ops, SparseCore 0:
  9.8 66.8 all-gather.2
  108.4 178.5 all-reduce.1
  288.8 53.8 all-gather.4
  348.7 87.4 reduce-scatter.1
where the time goes:
time: 445 us; the launch traced here: 444 us
  waiting for transfers between devices  294 us (66%)
  blocking collectives  82.3 us (18%)
  other arithmetic  27.7 us (6%)
  between operations  13.9 us (3%)
  local copies, waits for them, and re-layouts  11.1 us (2%)
  matrix products  10.7 us (2%)
  starting transfers between devices  4.67 us (1%)
    reduce_scatter x1, waiting for transfers between devices, per_device(): cross = lax.psum_scatter(product, 'dp', scatter_dimension=0, tiled=True)  86.4 us
    psum x1, waiting for transfers between devices, per_device(): totals, members = lax.psum((totals, members), 'dp')  84.2 us
    psum x1, blocking collectives, per_device(): totals, members = lax.psum((totals, members), 'dp')  82.3 us
    all_gather x1, waiting for transfers between devices, per_device(): lax.all_gather(rotation, 'sub', axis=1, tiled=True)  68.8 us
    all_gather x1, waiting for transfers between devices, per_device(): gathered = lax.all_gather(vectors, 'sub', axis=0, tiled=True)  45.2 us
    unnamed x5, other arithmetic  24.3 us
  transfers between devices with their start and end apart: 5, of which 5 were waited for; matrix products, arithmetic and copies ran while one was open for 5% of the time, Pallas kernels for 0%

commit v1 on v0

v1 whole, which is shorter than its diff:
```python
import jax
import jax.numpy as jnp
from jax import lax
from jax.experimental import pallas as pl
from jax.experimental.pallas import tpu as pltpu
from jax.sharding import PartitionSpec as P

BF16 = jnp.bfloat16
F32 = jnp.float32
MESH = pl.DeviceIdType.MESH

D = 2048
K = 4096
DS = 128
GROUP = 2048
OWN = 256
SEMS = 160


def kernel(
    v_ref, r_ref, cb_ref, codes_ref,
    cent_out, dist_ref, cross_ref,
    vg, rot, oth, rott, rown, roth, raw, codes, lo, hicol, counts, tacc, tsend, trecv, cnt, cbk, cent,
    reb, rebb, xf, xs, xr, zs, zr,
    ssem, rsem, lsem,
):
    dp = lax.axis_index("dp")
    sub = lax.axis_index("sub")
    zh, y = lax.div(dp, 4), lax.rem(dp, 4)
    x, zl, core = lax.div(sub, 4), lax.rem(lax.div(sub, 2), 2), lax.rem(sub, 2)
    xp, xm, x2 = lax.rem(x + 1, 4), lax.rem(x + 3, 4), lax.rem(x + 2, 4)
    yp, ym, y2 = lax.rem(y + 1, 4), lax.rem(y + 3, 4), lax.rem(y + 2, 4)
    zo, co = 1 - zl, 1 - core

    def sid(a, b, c):
        return a * 4 + b * 2 + c

    to_xp, to_xm = (dp, sid(xp, zl, core)), (dp, sid(xm, zl, core))
    to_z = (dp, sid(x, zo, core))
    to_core = (dp, sid(x, zl, co))
    to_out = (lax.rem(zh + 3 + 2 * zl, 4) * 4 + y, sid(x, zo, core))

    def to_y(k):
        return (zh * 4 + lax.rem(y + k, 4), sub)

    def to_zh(k):
        return (lax.rem(zh + k, 4) * 4 + y, sub)

    pending = []
    ids = {}

    def role(name):
        return ids.setdefault(name, len(ids))

    def send(name, src, dst, target):
        i = role(name)
        copy = pltpu.make_async_remote_copy(
            src_ref=src, dst_ref=dst, send_sem=ssem.at[i], recv_sem=rsem.at[i],
            device_id=target, device_id_type=MESH,
        )
        copy.start()
        pending.append(copy)

    def recv(name, ref):
        i = role(name)
        pltpu.make_async_remote_copy(
            src_ref=ref, dst_ref=ref, send_sem=ssem.at[i], recv_sem=rsem.at[i],
            device_id=to_core, device_id_type=MESH,
        ).wait_recv()

    def piece(cp, h, c):
        return pl.ds(pl.multiple_of(cp * 256 + h * 128 + c * 64, 64), 64)

    def unit(cp, h):
        return pl.ds(pl.multiple_of(cp * 256 + h * 128, 128), 128)

    def chip(cp):
        return pl.ds(pl.multiple_of(cp * 256, 256), 256)

    here, up, down, far = x * 2 + zl, xp * 2 + zl, xm * 2 + zl, x2 * 2 + zl
    here_z, up_z, down_z, far_z = x * 2 + zo, xp * 2 + zo, xm * 2 + zo, x2 * 2 + zo

    local = [
        pltpu.make_async_copy(v_ref.at[pl.ds(h * 64, 64)], vg.at[piece(here, h, core)], lsem.at[h])
        for h in range(2)
    ]
    local.append(pltpu.make_async_copy(codes_ref, raw, lsem.at[2]))
    local.append(pltpu.make_async_copy(r_ref, rown, lsem.at[3]))
    hi_own = 4 * y + zh
    own_rows = pl.ds(pl.multiple_of(hi_own * OWN, OWN), OWN)
    local.append(pltpu.make_async_copy(cb_ref.at[own_rows], cbk, lsem.at[4]))
    for copy in local:
        copy.start()

    barrier = pltpu.get_barrier_semaphore()
    peers = [to_xp, to_xm, to_z, to_core, to_out] + [to_y(k) for k in (1, 3, 2)] + [to_zh(k) for k in (1, 3, 2)]
    for peer in peers:
        pl.semaphore_signal(barrier, inc=1, device_id=peer, device_id_type=MESH)
    for copy in local:
        copy.wait()

    even, odd = raw[pl.ds(0, 8, stride=2), :], raw[pl.ds(1, 8, stride=2), :]
    first = lax.broadcasted_iota(jnp.int32, (8, 128), 1) < 64
    codes[y, 0:8, :] = jnp.where(first, even, pltpu.roll(odd, 64, 1))
    codes[y, 8:16, :] = jnp.where(first, pltpu.roll(even, 64, 1), odd)
    pl.semaphore_wait(barrier, len(peers))

    def vsend(name, cp, h, c, target):
        ref = vg.at[piece(cp, h, c)]
        send(name, ref, ref, target)

    def vrecv(name, cp, h, c):
        recv(name, vg.at[piece(cp, h, c)])

    vsend("xm0", here, 0, core, to_xp)
    vsend("xp1", here, 1, core, to_xm)
    top, low = pl.ds(0, 1024), pl.ds(1024, 1024)
    send("r_in", rown.at[top], roth.at[top], to_z)
    send("r_out", rown.at[low], roth.at[low], to_out)
    for h in range(2):
        vsend("d_own%d" % h, here, h, core, to_core)
    for k in (1, 3, 2):
        send("code%d" % k, codes.at[y], codes.at[y], to_y(k))
    vsend("xm1", here, 1, core, to_xp)
    vsend("xp0", here, 0, core, to_xm)

    def y_send(name, rows, direct):
        ref = rot.at[y, rows]
        send("a" + name, ref, ref, to_y(1))
        send("b" + name, ref, ref, to_y(3))
        if direct:
            send("c" + name, ref, ref, to_y(2))

    def halves(start, size):
        a = pl.ds(pl.multiple_of(start, 64), size)
        b = pl.ds(pl.multiple_of(start + size, 64), size)
        return a, b

    def y_forward(name, start, size):
        rows = pl.ds(pl.multiple_of(start, 128), size)
        a, b = halves(start, size // 2)
        recv("a" + name, rot.at[ym, rows])
        ref = rot.at[ym, a]
        send("c" + name, ref, ref, to_y(1))
        recv("b" + name, rot.at[yp, rows])
        ref = rot.at[yp, b]
        send("d" + name, ref, ref, to_y(3))

    def y_last(name, start, size, direct):
        if direct:
            rows = pl.ds(pl.multiple_of(start, 128), size)
            recv("a" + name, rot.at[ym, rows])
            recv("b" + name, rot.at[yp, rows])
            recv("c" + name, rot.at[y2, rows])
        else:
            a, b = halves(start, size // 2)
            recv("c" + name, rot.at[y2, a])
            recv("d" + name, rot.at[y2, b])

    def rot_own(rows):
        part = jnp.dot(vg[rows, :], rown[...], preferred_element_type=F32)
        rot[y, rows, :] = part.astype(BF16)

    def rot_oth(rows):
        part = jnp.dot(vg[rows, :], roth[...], preferred_element_type=F32)
        oth[rows, :] = part.astype(BF16)

    def rot_both(rows):
        both = jnp.concatenate([rown[...], roth[...]], axis=1)
        part = jnp.dot(vg[rows, :], both, preferred_element_type=F32)
        rot[y, rows, :] = part[:, :DS].astype(BF16)
        oth[rows, :] = part[:, DS:].astype(BF16)

    def z_send(name, rows):
        send("z" + name, oth.at[rows], rot.at[y, rows], to_z)

    def z_recv(name, rows):
        recv("z" + name, rot.at[y, rows])

    for h in range(2):
        vrecv("d_own%d" % h, here, h, co)
    rot_own(chip(here))
    y_send("A", chip(here), False)

    for k in (1, 3, 2):
        recv("code%d" % k, codes.at[lax.rem(y + 4 - k, 4)])
    tacc[...] = jnp.zeros_like(tacc)
    iota = lax.broadcasted_iota(jnp.int32, (256, 128), 0)

    def lo_table(g, carry):
        tile = jnp.bitwise_and(codes[g], 255)
        for i in range(16):
            cp, h = i // 2, i % 2
            row = tile[h * 8 + cp:h * 8 + cp + 1, :]
            mark = jnp.where(iota == jnp.broadcast_to(row, (256, 128)), 1.0, 0.0)
            lo[:, pl.ds(pl.multiple_of(g * GROUP + i * 128, 128), 128)] = mark.astype(BF16)
        return carry

    lax.fori_loop(0, 4, lo_table, 0)

    def hi_table(g, carry):
        tile = lax.shift_right_logical(codes[g], 8).astype(F32)
        for i in range(16):
            cp, h = i // 2, i % 2
            row = tile[h * 8 + cp:h * 8 + cp + 1, :]
            hicol[g, i * 128:(i + 1) * 128, :] = jnp.broadcast_to(row, (128, 128)).T.astype(BF16)
        return carry

    vrecv("xm0", down, 0, core)
    vsend("x20", down, 0, core, to_xp)
    vsend("d_xm0", down, 0, core, to_core)
    vrecv("xp1", up, 1, core)
    vsend("x21", up, 1, core, to_xm)
    vsend("d_xp1", up, 1, core, to_core)
    recv("r_in", roth.at[top])
    recv("r_out", roth.at[low])
    rot_oth(chip(here))
    z_send("A", chip(here))
    vrecv("d_xm0", down, 0, co)
    rot_both(unit(down, 0))
    y_send("B", unit(down, 0), False)
    z_send("B", unit(down, 0))
    vrecv("d_xp1", up, 1, co)
    rot_both(unit(up, 1))
    y_send("C", unit(up, 1), False)
    z_send("C", unit(up, 1))
    vsend("w0", here, 0, core, to_z)
    y_forward("A", here * 256, 256)
    lax.fori_loop(0, 4, hi_table, 0)

    z_recv("A", chip(here_z))
    y_send("Az", chip(here_z), False)
    z_recv("B", unit(down_z, 0))
    y_send("Bz", unit(down_z, 0), False)
    z_recv("C", unit(up_z, 1))
    y_send("Cz", unit(up_z, 1), False)
    y_forward("B", down * 256, 128)
    y_forward("C", up * 256 + 128, 128)

    def count(g, acc):
        for h in range(2):
            for cp in range(8):
                row = lax.shift_right_logical(codes[g, h * 8 + cp:h * 8 + cp + 1, :], 8)
                mark = jnp.where(iota[:16] == jnp.broadcast_to(row, (16, 128)), 1.0, 0.0).astype(BF16)
                tab = lo[:, pl.ds(pl.multiple_of(g * GROUP + (cp * 2 + h) * 128, 128), 128)]
                acc = acc + lax.dot_general(mark, tab, (((1,), (1,)), ((), ())), preferred_element_type=F32)
        return acc

    counts[0] = lax.fori_loop(0, 4, count, jnp.zeros((16, 256), F32))
    for k in (1, 3, 2):
        send("n%d" % k, counts.at[0], counts.at[k], to_zh(k))

    vrecv("xm1", down, 1, core)
    vsend("d_xm1", down, 1, core, to_core)
    vrecv("xp0", up, 0, core)
    vsend("d_xp0", up, 0, core, to_core)
    vrecv("d_xm1", down, 1, co)
    rot_both(unit(down, 1))
    y_send("D", unit(down, 1), False)
    z_send("D", unit(down, 1))
    vrecv("d_xp0", up, 0, co)
    rot_both(unit(up, 0))
    y_send("E", unit(up, 0), False)
    z_send("E", unit(up, 0))
    vsend("w1", here, 1, core, to_z)
    y_forward("Az", here_z * 256, 256)
    y_forward("Bz", down_z * 256, 128)
    y_forward("Cz", up_z * 256 + 128, 128)

    def accumulate(cp):
        def body(g, carry):
            marks = lo[:, pl.ds(pl.multiple_of(g * GROUP + cp * 256, 256), 256)]
            values = rot[g, chip(cp), :]
            his = hicol[g, chip(cp), :]
            parts = []
            for h in range(4):
                want = (4 * y + h).astype(F32).astype(BF16)
                parts.append(jnp.where(his == want, values, jnp.zeros_like(values)))
            wide = jnp.concatenate(parts, axis=1)
            tacc[...] += jnp.dot(marks, wide, preferred_element_type=F32)
            return carry

        lax.fori_loop(0, 4, body, 0)

    y_last("A", here * 256, 256, False)
    accumulate(here)
    z_recv("D", unit(down_z, 1))
    y_send("Dz", unit(down_z, 1), False)
    z_recv("E", unit(up_z, 0))
    y_send("Ez", unit(up_z, 0), False)
    y_forward("D", down * 256 + 128, 128)
    y_forward("E", up * 256, 128)
    y_last("Az", here_z * 256, 256, False)
    accumulate(here_z)

    vrecv("x20", far, 0, core)
    vsend("d_x20", far, 0, core, to_core)
    vrecv("x21", far, 1, core)
    vsend("d_x21", far, 1, core, to_core)
    for h in range(2):
        vrecv("d_x2%d" % h, far, h, co)
    rot_both(chip(far))
    z_send("F", chip(far))
    y_send("F", chip(far), True)
    y_forward("Dz", down_z * 256 + 128, 128)
    y_forward("Ez", up_z * 256, 128)

    vrecv("w0", here_z, 0, core)
    vsend("wm0", here_z, 0, core, to_xp)
    vsend("wp0", here_z, 0, core, to_xm)
    vsend("d_w0", here_z, 0, core, to_core)
    z_recv("F", chip(far_z))
    y_send("Fz", chip(far_z), True)
    y_last("B", down * 256, 128, False)
    y_last("D", down * 256 + 128, 128, False)
    accumulate(down)
    y_last("C", up * 256 + 128, 128, False)
    y_last("E", up * 256, 128, False)
    accumulate(up)
    vrecv("w1", here_z, 1, core)
    vsend("wp1", here_z, 1, core, to_xm)
    vsend("wm1", here_z, 1, core, to_xp)
    vsend("d_w1", here_z, 1, core, to_core)
    y_last("Bz", down_z * 256, 128, False)
    y_last("Dz", down_z * 256 + 128, 128, False)
    accumulate(down_z)
    y_last("Cz", up_z * 256 + 128, 128, False)
    y_last("Ez", up_z * 256, 128, False)
    accumulate(up_z)
    y_last("F", far * 256, 256, True)
    accumulate(far)
    y_last("Fz", far_z * 256, 256, True)
    accumulate(far_z)

    for k in (2, 1, 3):
        theirs = pl.ds(pl.multiple_of(lax.rem(zh + k, 4) * DS, DS), DS)
        tsend[k - 1] = tacc[:, theirs].astype(BF16)
        send("t%d" % k, tsend.at[k - 1], trecv.at[k - 1], to_zh(k))
    for k in (1, 3, 2):
        recv("n%d" % k, counts.at[k])
    number = counts[0] + counts[1] + counts[2] + counts[3]
    counts[4] = number
    mine = counts[4, pl.ds(hi_own, 1), :]
    cnt[...] = jnp.broadcast_to(mine, (128, 256)).T
    rott[...] = rot[y].astype(F32).T
    vrecv("wm0", down_z, 0, core)
    vsend("w20", down_z, 0, core, to_xp)
    vsend("d_wm0", down_z, 0, core, to_core)
    vrecv("wp1", up_z, 1, core)
    vsend("w21", up_z, 1, core, to_xm)
    vsend("d_wp1", up_z, 1, core, to_core)
    total = tacc[:, pl.ds(pl.multiple_of(zh * DS, DS), DS)]
    for k in (1, 3, 2):
        recv("t%d" % k, trecv.at[k - 1])
        total = total + trecv[k - 1].astype(F32)
    cent[own_rows, :] = ((total + cbk[...].astype(F32)) / (cnt[...] + 1.0)).astype(BF16)

    def chunk(a, b):
        return pl.ds(pl.multiple_of(b * 1024 + a * OWN, OWN), OWN)

    def half_chunk(a, b, h):
        return pl.ds(pl.multiple_of(b * 1024 + a * OWN + h * 128, 128), 128)

    outs = []

    def rebuild(a, b):
        copy = pltpu.make_async_copy(
            cent.at[chunk(a, b)], cent_out.at[chunk(a, b)], lsem.at[5 + len(outs)]
        )
        copy.start()
        outs.append(copy)
        table = cent[chunk(a, b), :].astype(F32).T.astype(BF16)
        want = 4 * b + a

        def body(i, carry):
            tab = lo[:, pl.ds(pl.multiple_of(y * GROUP + i * 256, 256), 256)]
            got = jnp.dot(table, tab, preferred_element_type=F32)
            place = pl.ds(pl.multiple_of(i * 256, 256), 256)
            row = jnp.concatenate([codes[y, pl.ds(i, 1), :], codes[y, pl.ds(i + 8, 1), :]], axis=1)
            hit = lax.shift_right_logical(row, 8) == want
            reb[:, place] = jnp.where(jnp.broadcast_to(hit, (128, 256)), got, reb[:, place])
            return carry

        lax.fori_loop(0, 8, body, 0)

    def y_chunk_send(q, a):
        ref = cent.at[chunk(a, y)]
        send("ca%d" % q, ref, ref, to_y(1))
        send("cb%d" % q, ref, ref, to_y(3))

    def y_chunk_forward(q, a):
        recv("ca%d" % q, cent.at[chunk(a, ym)])
        ref = cent.at[half_chunk(a, ym, 0)]
        send("cc%d" % q, ref, ref, to_y(1))
        recv("cb%d" % q, cent.at[chunk(a, yp)])
        ref = cent.at[half_chunk(a, yp, 1)]
        send("cd%d" % q, ref, ref, to_y(3))

    reb[...] = jnp.zeros_like(reb)
    zs_of = [zh] + [lax.rem(zh + 4 - q, 4) for q in (1, 2, 3)]
    for k in (2, 1, 3):
        ref = cent.at[own_rows]
        send("cz%d" % k, ref, ref, to_zh(k))
    y_chunk_send(0, zh)
    rebuild(zh, y)
    y_chunk_forward(0, zh)
    order = (1, 3, 2)
    before = 0
    for q in order:
        a = zs_of[q]
        recv("cz%d" % q, cent.at[chunk(a, y)])
        y_chunk_send(q, a)
        if before:
            y_chunk_forward(before, zs_of[before])
        rebuild(a, y)
        rebuild(zs_of[before], ym)
        rebuild(zs_of[before], yp)
        before = q
    y_chunk_forward(before, zs_of[before])
    for b in (ym, yp):
        rebuild(zs_of[before], b)

    vrecv("wm1", down_z, 1, core)
    vsend("d_wm1", down_z, 1, core, to_core)
    vrecv("wp0", up_z, 0, core)
    vsend("d_wp0", up_z, 0, core, to_core)
    vrecv("w20", far_z, 0, core)
    vsend("d_w20", far_z, 0, core, to_core)
    vrecv("w21", far_z, 1, core)
    vsend("d_w21", far_z, 1, core, to_core)
    for q in (0,) + order:
        a = zs_of[q]
        recv("cc%d" % q, cent.at[half_chunk(a, y2, 0)])
        recv("cd%d" % q, cent.at[half_chunk(a, y2, 1)])
        rebuild(a, y2)
    for h in range(2):
        vrecv("d_w%d" % h, here_z, h, co)
        vrecv("d_wm%d" % h, down_z, h, co)
        vrecv("d_wp%d" % h, up_z, h, co)
        vrecv("d_w2%d" % h, far_z, h, co)

    rebb[...] = reb[...].astype(BF16)

    def cross_half(p):
        def body(i, carry):
            place = pl.ds(pl.multiple_of(i * 512 + p * 256, 256), 256)
            part = jnp.dot(rebb[...], vg[:, place], preferred_element_type=F32)
            xf[2 * p, i] = part[:, :128]
            xf[2 * p + 1, i] = part[:, 128:]
            return carry

        lax.fori_loop(0, 4, body, 0)

    def cross_send(k):
        xs[k - 1] = xf[lax.rem(y + k, 4)].astype(BF16)
        send("xa%d" % k, xs.at[k - 1], xr.at[k - 1], to_y(k))

    near = lax.div(y, 2)
    cross_half(1 - near)
    cross_send(2)
    cross_half(near)
    cross_send(1)
    cross_send(3)

    gap = rott[...] - reb[...]
    gap = jnp.sum(gap * gap, axis=0, keepdims=True)
    half_row = lax.broadcasted_iota(jnp.int32, (1, 128), 1) < 64
    for cp in range(8):
        u0, u1 = gap[:, cp * 256:cp * 256 + 128], gap[:, cp * 256 + 128:cp * 256 + 256]
        dist_ref[2 * cp:2 * cp + 1, :] = jnp.where(half_row, u0, pltpu.roll(u1, 64, 1))
        dist_ref[2 * cp + 1:2 * cp + 2, :] = jnp.where(half_row, pltpu.roll(u0, 64, 1), u1)

    for k in (1, 3, 2):
        recv("xa%d" % k, xr.at[k - 1])
    xf[y] = xf[y] + xr[0].astype(F32) + xr[1].astype(F32) + xr[2].astype(F32)
    for k in (2, 1, 3):
        zs[k - 1] = xf[y, lax.rem(zh + k, 4)].astype(BF16)
        send("xz%d" % k, zs.at[k - 1], zr.at[k - 1], to_zh(k))
    out = xf[y, zh]
    for k in (1, 3, 2):
        recv("xz%d" % k, zr.at[k - 1])
        out = out + zr[k - 1].astype(F32)
    cross_ref[...] = out.T

    for copy in outs:
        copy.wait()
    for copy in pending:
        copy.wait_send()


def per_device(vectors, rotation, codebook, codes):
    vmem = pl.BlockSpec(memory_space=pltpu.VMEM)
    hbm = pl.BlockSpec(memory_space=pltpu.HBM)
    cent, dist, cross = pl.pallas_call(
        kernel,
        out_shape=(
            jax.ShapeDtypeStruct((K, DS), BF16),
            jax.ShapeDtypeStruct((16, 128), F32),
            jax.ShapeDtypeStruct((DS, DS), F32),
        ),
        in_specs=[hbm] * 4,
        out_specs=(pl.BlockSpec(memory_space=pl.ANY), vmem, vmem),
        scratch_shapes=[
            pltpu.VMEM((GROUP, D), BF16),
            pltpu.VMEM((4, GROUP, DS), BF16),
            pltpu.VMEM((GROUP, DS), BF16),
            pltpu.VMEM((DS, GROUP), F32),
            pltpu.VMEM((D, DS), BF16),
            pltpu.VMEM((D, DS), BF16),
            pltpu.VMEM((16, 128), jnp.int32),
            pltpu.VMEM((4, 16, 128), jnp.int32),
            pltpu.VMEM((256, 4 * GROUP), BF16),
            pltpu.VMEM((4, GROUP, DS), BF16),
            pltpu.VMEM((5, 16, 256), F32),
            pltpu.VMEM((256, 4 * DS), F32),
            pltpu.VMEM((3, OWN, DS), BF16),
            pltpu.VMEM((3, OWN, DS), BF16),
            pltpu.VMEM((OWN, DS), F32),
            pltpu.VMEM((OWN, DS), BF16),
            pltpu.VMEM((K, DS), BF16),
            pltpu.VMEM((DS, GROUP), F32),
            pltpu.VMEM((DS, GROUP), BF16),
            pltpu.VMEM((4, 4, DS, 128), F32),
            pltpu.VMEM((3, 4, DS, 128), BF16),
            pltpu.VMEM((3, 4, DS, 128), BF16),
            pltpu.VMEM((3, DS, 128), BF16),
            pltpu.VMEM((3, DS, 128), BF16),
            pltpu.SemaphoreType.DMA((SEMS,)),
            pltpu.SemaphoreType.DMA((SEMS,)),
            pltpu.SemaphoreType.DMA((21,)),
        ],
        compiler_params=pltpu.CompilerParams(
            collective_id=0, has_side_effects=True, vmem_limit_bytes=48 * 1024 * 1024
        ),
        name="opq_step",
    )(vectors, rotation, codebook.reshape(K, DS), codes.reshape(16, 128))
    return cent.reshape(1, K, DS), dist.reshape(GROUP, 1), cross


def solution(mesh):
    placed = (P(("dp", "sub"), None), P(None, "sub"), P("sub", None, None), P("dp", "sub"))
    return jax.shard_map(
        per_device,
        mesh=mesh,
        in_specs=placed,
        out_specs=(P("sub", None, None), P("dp", "sub"), P("dp", "sub")),
        check_vma=False,
    )
```

time: 445 us -> 110 us (0.25)
  the two profiles are of different devices: /device:TPU:2 before, /device:TPU:1 now
where the time goes in v1:
time: 110 us
  Pallas kernels  103 us (94%)
  local copies, waits for them, and re-layouts  6.2 us (6%)
    pallas_call x1, Pallas kernels, per_device(): pl.pallas_call(kernel, out_shape=(jax.ShapeDtypeStruct((K, DS), BF16), ja...  103 us
    unnamed x11, local copies, waits for them, and re-layouts  6.2 us

profile of v1, /device:TPU:1, one launch (start us, length us, event | category | flops | bytes accessed | tf_op | source)
XLA Modules:
  0.0 110.0 jit_solution(1044091425343616062)
XLA Ops:
  0.6 0.0 copy-start
  0.6 1.2 %copy-done = bf16[1,4096,128]{2,1,0:T(8,128)(2,1)S(1)} copy-done((bf16[1,4096,128]{2,1,0:T(8,128)(2,1)S(1)}, bf16[1,4096,128]{2,1,0:T(8,128)(2,1)}, u32[]{:S(2)}) %copy-start) | copy-done | bytes 1048600
  1.9 0.0 copy-start.1
  1.9 1.0 copy-done.1
  2.9 0.0 copy-start.2
  2.9 1.0 copy-done.2
  3.9 0.0 copy-start.3
  3.9 0.7 copy-done.3
  4.6 103.2 %opq_step.1 = (bf16[4096,128]{1,0:T(8,128)(2,1)S(1)}, f32[16,128]{1,0:T(8,128)S(1)}, f32[128,128]{1,0:T(8,128)S(1)}) custom-call(bf16[128,2048]{1,0:T(8,128)(2,1)S(1)} %copy-done.1, bf16[2048,128]{1,0:T(8,128)(2,1)S(1)} %copy-done.2, bf16[4096,128]{1,0:T(8,128)(2,1)S(1)} %bitcast.4, s32[16,128]{1,0:T(8,128)S(1)} %bitcast.6), custom_call_target="tpu_custom_call" | custom-call | tf_op jit(solution)/shard_map/opq_step/pallas_call | solution.py:494
  107.8 1.0 copy.10
  108.8 0.6 copy.11
  109.4 0.6 copy.12
Async XLA Ops:
  0.6 1.2 %copy-start = (bf16[1,4096,128]{2,1,0:T(8,128)(2,1)S(1)}, bf16[1,4096,128]{2,1,0:T(8,128)(2,1)}, u32[]{:S(2)}) copy-start(bf16[1,4096,128]{2,1,0:T(8,128)(2,1)} %param.6) | copy-start | bytes 3145732
  1.9 1.0 copy-start.1
  2.9 1.0 copy-start.2
  3.9 0.7 copy-start.3

commit v2 on v1

--- a/solution.py
+++ b/solution.py
@@ -268,19 +268,18 @@
     y_forward("Cz", up_z * 256 + 128, 128)
 
     def accumulate(cp):
-        def body(g, carry):
-            marks = lo[:, pl.ds(pl.multiple_of(g * GROUP + cp * 256, 256), 256)]
+        marks, wides = [], []
+        for g in range(4):
+            marks.append(lo[:, pl.ds(pl.multiple_of(g * GROUP + cp * 256, 256), 256)])
             values = rot[g, chip(cp), :]
             his = hicol[g, chip(cp), :]
             parts = []
             for h in range(4):
                 want = (4 * y + h).astype(F32).astype(BF16)
                 parts.append(jnp.where(his == want, values, jnp.zeros_like(values)))
-            wide = jnp.concatenate(parts, axis=1)
-            tacc[...] += jnp.dot(marks, wide, preferred_element_type=F32)
-            return carry
-
-        lax.fori_loop(0, 4, body, 0)
+            wides.append(jnp.concatenate(parts, axis=1))
+        mark, wide = jnp.concatenate(marks, axis=1), jnp.concatenate(wides, axis=0)
+        tacc[...] += jnp.dot(mark, wide, preferred_element_type=F32)
 
     y_last("A", here * 256, 256, False)
     accumulate(here)
@@ -371,17 +370,13 @@
         outs.append(copy)
         table = cent[chunk(a, b), :].astype(F32).T.astype(BF16)
         want = 4 * b + a
-
-        def body(i, carry):
+        for i in range(8):
             tab = lo[:, pl.ds(pl.multiple_of(y * GROUP + i * 256, 256), 256)]
             got = jnp.dot(table, tab, preferred_element_type=F32)
-            place = pl.ds(pl.multiple_of(i * 256, 256), 256)
-            row = jnp.concatenate([codes[y, pl.ds(i, 1), :], codes[y, pl.ds(i + 8, 1), :]], axis=1)
+            place = slice(i * 256, (i + 1) * 256)
+            row = jnp.concatenate([codes[y, i:i + 1, :], codes[y, i + 8:i + 9, :]], axis=1)
             hit = lax.shift_right_logical(row, 8) == want
             reb[:, place] = jnp.where(jnp.broadcast_to(hit, (128, 256)), got, reb[:, place])
-            return carry
-
-        lax.fori_loop(0, 8, body, 0)
 
     def y_chunk_send(q, a):
         ref = cent.at[chunk(a, y)]
@@ -491,6 +486,7 @@
 def per_device(vectors, rotation, codebook, codes):
     vmem = pl.BlockSpec(memory_space=pltpu.VMEM)
     hbm = pl.BlockSpec(memory_space=pltpu.HBM)
+    operands = (vectors, rotation, codebook.reshape(K, DS), codes.reshape(16, 128))
     cent, dist, cross = pl.pallas_call(
         kernel,
         out_shape=(
@@ -533,7 +529,7 @@
             collective_id=0, has_side_effects=True, vmem_limit_bytes=48 * 1024 * 1024
         ),
         name="opq_step",
-    )(vectors, rotation, codebook.reshape(K, DS), codes.reshape(16, 128))
+    )(*(pltpu.with_memory_space_constraint(t, pltpu.HBM) for t in operands))
     return cent.reshape(1, K, DS), dist.reshape(GROUP, 1), cross
 
 

time: 110 us -> 95.4 us (0.87)
  Pallas kernels: 103 us -> 92.5 us
  local copies, waits for them, and re-layouts: 6.2 us -> 2.2 us
    pallas_call x1, Pallas kernels: 103 us -> 92.5 us  [per_device(): pl.pallas_call(kernel, out_shape=(jax.ShapeDtypeStruct((K, DS), BF16), ja...]
    unnamed x11 -> x3, local copies, waits for them, and re-layouts: 6.2 us -> 2.2 us
where the time goes in v2:
time: 95.4 us; the launch traced here: 95.3 us
  Pallas kernels  92.5 us (97%)
  local copies, waits for them, and re-layouts  2.2 us (2%)
    pallas_call x1, Pallas kernels, per_device(): pl.pallas_call(kernel, out_shape=(jax.ShapeDtypeStruct((K, DS), BF16), ja...  92.5 us
    unnamed x3, local copies, waits for them, and re-layouts  2.2 us

profile of v2, /device:TPU:1, one launch (start us, length us, event | category | flops | bytes accessed | tf_op | source)
XLA Modules:
  0.0 95.3 jit_solution(7710340163758369017)
XLA Ops:
  0.6 92.5 %opq_step.1 = (bf16[4096,128]{1,0:T(8,128)(2,1)S(1)}, f32[16,128]{1,0:T(8,128)S(1)}, f32[128,128]{1,0:T(8,128)S(1)}) custom-call(bf16[128,2048]{1,0:T(8,128)(2,1)} %v_ref.1, bf16[2048,128]{1,0:T(8,128)(2,1)} %r_ref.1, bf16[4096,128]{1,0:T(8,128)(2,1)} %bitcast.6, s32[16,128]{1,0:T(8,128)} %bitcast.7), custom_call_target="tpu_custom_call" | custom-call | tf_op jit(solution)/shard_map/opq_step/pallas_call | solution.py:490
  93.1 1.0 %copy.10 = bf16[1,4096,128]{2,1,0:T(8,128)(2,1)} copy(bf16[1,4096,128]{2,1,0:T(8,128)(2,1)S(1)} %bitcast.4) | data formatting | bytes 2097152
  94.1 0.6 copy.11
  94.7 0.6 copy.12

commit v3 on v2

--- a/solution.py
+++ b/solution.py
@@ -14,7 +14,7 @@
 DS = 128
 GROUP = 2048
 OWN = 256
-SEMS = 160
+SEMS = 192
 
 
 def kernel(
@@ -113,7 +113,7 @@
         recv(name, vg.at[piece(cp, h, c)])
 
     vsend("xm0", here, 0, core, to_xp)
-    vsend("xp1", here, 1, core, to_xm)
+    vsend("xp0", here, 0, core, to_xm)
     top, low = pl.ds(0, 1024), pl.ds(1024, 1024)
     send("r_in", rown.at[top], roth.at[top], to_z)
     send("r_out", rown.at[low], roth.at[low], to_out)
@@ -122,7 +122,26 @@
     for k in (1, 3, 2):
         send("code%d" % k, codes.at[y], codes.at[y], to_y(k))
     vsend("xm1", here, 1, core, to_xp)
-    vsend("xp0", here, 0, core, to_xm)
+    vsend("xp1", here, 1, core, to_xm)
+
+    def quarter(cp, h, v, c):
+        return vg.at[pl.ds(pl.multiple_of(cp * 256 + h * 128 + c * 64 + v * 32, 32), 32)]
+
+    def x_forward(h):
+        vrecv("xm%d" % h, down, h, core)
+        ref = quarter(down, h, 0, core)
+        send("xf%d" % h, ref, ref, to_xp)
+        vsend("d_xm%d" % h, down, h, core, to_core)
+        vrecv("xp%d" % h, up, h, core)
+        ref = quarter(up, h, 1, core)
+        send("xg%d" % h, ref, ref, to_xm)
+        vsend("d_xp%d" % h, up, h, core, to_core)
+
+    def x_far(h):
+        recv("xf%d" % h, quarter(far, h, 0, core))
+        recv("xg%d" % h, quarter(far, h, 1, core))
+        vsend("d_x2%d" % h, far, h, core, to_core)
+        vrecv("d_x2%d" % h, far, h, co)
 
     def y_send(name, rows, direct):
         ref = rot.at[y, rows]
@@ -206,12 +225,7 @@
             hicol[g, i * 128:(i + 1) * 128, :] = jnp.broadcast_to(row, (128, 128)).T.astype(BF16)
         return carry
 
-    vrecv("xm0", down, 0, core)
-    vsend("x20", down, 0, core, to_xp)
-    vsend("d_xm0", down, 0, core, to_core)
-    vrecv("xp1", up, 1, core)
-    vsend("x21", up, 1, core, to_xm)
-    vsend("d_xp1", up, 1, core, to_core)
+    x_forward(0)
     recv("r_in", roth.at[top])
     recv("r_out", roth.at[low])
     rot_oth(chip(here))
@@ -220,11 +234,10 @@
     rot_both(unit(down, 0))
     y_send("B", unit(down, 0), False)
     z_send("B", unit(down, 0))
-    vrecv("d_xp1", up, 1, co)
-    rot_both(unit(up, 1))
-    y_send("C", unit(up, 1), False)
-    z_send("C", unit(up, 1))
-    vsend("w0", here, 0, core, to_z)
+    vrecv("d_xp0", up, 0, co)
+    rot_both(unit(up, 0))
+    y_send("C", unit(up, 0), False)
+    z_send("C", unit(up, 0))
     y_forward("A", here * 256, 256)
     lax.fori_loop(0, 4, hi_table, 0)
 
@@ -232,10 +245,10 @@
     y_send("Az", chip(here_z), False)
     z_recv("B", unit(down_z, 0))
     y_send("Bz", unit(down_z, 0), False)
-    z_recv("C", unit(up_z, 1))
-    y_send("Cz", unit(up_z, 1), False)
+    z_recv("C", unit(up_z, 0))
+    y_send("Cz", unit(up_z, 0), False)
     y_forward("B", down * 256, 128)
-    y_forward("C", up * 256 + 128, 128)
+    y_forward("C", up * 256, 128)
 
     def count(g, acc):
         for h in range(2):
@@ -250,22 +263,18 @@
     for k in (1, 3, 2):
         send("n%d" % k, counts.at[0], counts.at[k], to_zh(k))
 
-    vrecv("xm1", down, 1, core)
-    vsend("d_xm1", down, 1, core, to_core)
-    vrecv("xp0", up, 0, core)
-    vsend("d_xp0", up, 0, core, to_core)
+    x_forward(1)
     vrecv("d_xm1", down, 1, co)
     rot_both(unit(down, 1))
     y_send("D", unit(down, 1), False)
     z_send("D", unit(down, 1))
-    vrecv("d_xp0", up, 0, co)
-    rot_both(unit(up, 0))
-    y_send("E", unit(up, 0), False)
-    z_send("E", unit(up, 0))
-    vsend("w1", here, 1, core, to_z)
+    vrecv("d_xp1", up, 1, co)
+    rot_both(unit(up, 1))
+    y_send("E", unit(up, 1), False)
+    z_send("E", unit(up, 1))
     y_forward("Az", here_z * 256, 256)
     y_forward("Bz", down_z * 256, 128)
-    y_forward("Cz", up_z * 256 + 128, 128)
+    y_forward("Cz", up_z * 256, 128)
 
     def accumulate(cp):
         marks, wides = [], []
@@ -283,82 +292,112 @@
 
     y_last("A", here * 256, 256, False)
     accumulate(here)
+    x_far(0)
+    rot_both(unit(far, 0))
+    z_send("F", unit(far, 0))
+    y_send("F", unit(far, 0), True)
     z_recv("D", unit(down_z, 1))
     y_send("Dz", unit(down_z, 1), False)
-    z_recv("E", unit(up_z, 0))
-    y_send("Ez", unit(up_z, 0), False)
+    z_recv("E", unit(up_z, 1))
+    y_send("Ez", unit(up_z, 1), False)
     y_forward("D", down * 256 + 128, 128)
-    y_forward("E", up * 256, 128)
+    y_forward("E", up * 256 + 128, 128)
+
+    x_far(1)
+    rot_both(unit(far, 1))
+    z_send("G", unit(far, 1))
+    y_send("G", unit(far, 1), True)
+    vsend("w0", here, 0, core, to_z)
+    vsend("w1", here, 1, core, to_z)
+    z_recv("F", unit(far_z, 0))
+    y_send("Fz", unit(far_z, 0), True)
+    y_forward("Dz", down_z * 256 + 128, 128)
+    y_forward("Ez", up_z * 256 + 128, 128)
+    z_recv("G", unit(far_z, 1))
+    y_send("Gz", unit(far_z, 1), True)
     y_last("Az", here_z * 256, 256, False)
     accumulate(here_z)
-
-    vrecv("x20", far, 0, core)
-    vsend("d_x20", far, 0, core, to_core)
-    vrecv("x21", far, 1, core)
-    vsend("d_x21", far, 1, core, to_core)
-    for h in range(2):
-        vrecv("d_x2%d" % h, far, h, co)
-    rot_both(chip(far))
-    z_send("F", chip(far))
-    y_send("F", chip(far), True)
-    y_forward("Dz", down_z * 256 + 128, 128)
-    y_forward("Ez", up_z * 256, 128)
-
+    y_last("B", down * 256, 128, False)
+    y_last("D", down * 256 + 128, 128, False)
+    accumulate(down)
+    y_last("C", up * 256, 128, False)
+    y_last("E", up * 256 + 128, 128, False)
+    accumulate(up)
+    y_last("Bz", down_z * 256, 128, False)
+    y_last("Dz", down_z * 256 + 128, 128, False)
+    accumulate(down_z)
+    y_last("Cz", up_z * 256, 128, False)
+    y_last("Ez", up_z * 256 + 128, 128, False)
+    accumulate(up_z)
     vrecv("w0", here_z, 0, core)
     vsend("wm0", here_z, 0, core, to_xp)
     vsend("wp0", here_z, 0, core, to_xm)
     vsend("d_w0", here_z, 0, core, to_core)
-    z_recv("F", chip(far_z))
-    y_send("Fz", chip(far_z), True)
-    y_last("B", down * 256, 128, False)
-    y_last("D", down * 256 + 128, 128, False)
-    accumulate(down)
-    y_last("C", up * 256 + 128, 128, False)
-    y_last("E", up * 256, 128, False)
-    accumulate(up)
+    y_last("F", far * 256, 128, True)
+    y_last("G", far * 256 + 128, 128, True)
+    accumulate(far)
+    y_last("Fz", far_z * 256, 128, True)
+    y_last("Gz", far_z * 256 + 128, 128, True)
+    accumulate(far_z)
+
+    def part(hb):
+        return pl.ds(hb * 128, 128)
+
+    for hb in range(2):
+        for k in (2, 1, 3):
+            theirs = pl.ds(pl.multiple_of(lax.rem(zh + k, 4) * DS, DS), DS)
+            tsend[k - 1, part(hb), :] = tacc[part(hb), theirs].astype(BF16)
+            send("t%d%d" % (k, hb), tsend.at[k - 1, part(hb)], trecv.at[k - 1, part(hb)], to_zh(k))
+    for k in (1, 3, 2):
+        recv("n%d" % k, counts.at[k])
+    counts[4] = counts[0] + counts[1] + counts[2] + counts[3]
+    mine = counts[4, pl.ds(hi_own, 1), :]
+    cnt[...] = jnp.broadcast_to(mine, (128, 256)).T
+    rott[...] = rot[y].astype(F32).T
     vrecv("w1", here_z, 1, core)
     vsend("wp1", here_z, 1, core, to_xm)
     vsend("wm1", here_z, 1, core, to_xp)
     vsend("d_w1", here_z, 1, core, to_core)
-    y_last("Bz", down_z * 256, 128, False)
-    y_last("Dz", down_z * 256 + 128, 128, False)
-    accumulate(down_z)
-    y_last("Cz", up_z * 256 + 128, 128, False)
-    y_last("Ez", up_z * 256, 128, False)
-    accumulate(up_z)
-    y_last("F", far * 256, 256, True)
-    accumulate(far)
-    y_last("Fz", far_z * 256, 256, True)
-    accumulate(far_z)
-
-    for k in (2, 1, 3):
-        theirs = pl.ds(pl.multiple_of(lax.rem(zh + k, 4) * DS, DS), DS)
-        tsend[k - 1] = tacc[:, theirs].astype(BF16)
-        send("t%d" % k, tsend.at[k - 1], trecv.at[k - 1], to_zh(k))
-    for k in (1, 3, 2):
-        recv("n%d" % k, counts.at[k])
-    number = counts[0] + counts[1] + counts[2] + counts[3]
-    counts[4] = number
-    mine = counts[4, pl.ds(hi_own, 1), :]
-    cnt[...] = jnp.broadcast_to(mine, (128, 256)).T
-    rott[...] = rot[y].astype(F32).T
-    vrecv("wm0", down_z, 0, core)
-    vsend("w20", down_z, 0, core, to_xp)
-    vsend("d_wm0", down_z, 0, core, to_core)
-    vrecv("wp1", up_z, 1, core)
-    vsend("w21", up_z, 1, core, to_xm)
-    vsend("d_wp1", up_z, 1, core, to_core)
-    total = tacc[:, pl.ds(pl.multiple_of(zh * DS, DS), DS)]
-    for k in (1, 3, 2):
-        recv("t%d" % k, trecv.at[k - 1])
-        total = total + trecv[k - 1].astype(F32)
-    cent[own_rows, :] = ((total + cbk[...].astype(F32)) / (cnt[...] + 1.0)).astype(BF16)
 
     def chunk(a, b):
         return pl.ds(pl.multiple_of(b * 1024 + a * OWN, OWN), OWN)
 
-    def half_chunk(a, b, h):
-        return pl.ds(pl.multiple_of(b * 1024 + a * OWN + h * 128, 128), 128)
+    def half_chunk(a, b, hb):
+        return pl.ds(pl.multiple_of(b * 1024 + a * OWN + hb * 128, 128), 128)
+
+    def quarter_chunk(a, b, hb, v):
+        return pl.ds(pl.multiple_of(b * 1024 + a * OWN + hb * 128 + v * 64, 64), 64)
+
+    def y_chunk_send(q, hb):
+        ref = cent.at[half_chunk(zs_of[q], y, hb)]
+        send("ca%d%d" % (q, hb), ref, ref, to_y(1))
+        send("cb%d%d" % (q, hb), ref, ref, to_y(3))
+
+    def y_chunk_forward(q, hb):
+        a = zs_of[q]
+        recv("ca%d%d" % (q, hb), cent.at[half_chunk(a, ym, hb)])
+        ref = cent.at[quarter_chunk(a, ym, hb, 0)]
+        send("cc%d%d" % (q, hb), ref, ref, to_y(1))
+        recv("cb%d%d" % (q, hb), cent.at[half_chunk(a, yp, hb)])
+        ref = cent.at[quarter_chunk(a, yp, hb, 1)]
+        send("cd%d%d" % (q, hb), ref, ref, to_y(3))
+
+    def z_chunk(q, hb):
+        recv("cz%d%d" % (q, hb), cent.at[half_chunk(zs_of[q], y, hb)])
+        y_chunk_send(q, hb)
+
+    zs_of = [zh] + [lax.rem(zh + 4 - q, 4) for q in (1, 2, 3)]
+    for hb in range(2):
+        total = tacc[part(hb), pl.ds(pl.multiple_of(zh * DS, DS), DS)]
+        for k in (1, 3, 2):
+            recv("t%d%d" % (k, hb), trecv.at[k - 1, part(hb)])
+            total = total + trecv[k - 1, part(hb), :].astype(F32)
+        value = (total + cbk[part(hb), :].astype(F32)) / (cnt[part(hb), :] + 1.0)
+        cent[half_chunk(zh, y, hb), :] = value.astype(BF16)
+        ref = cent.at[half_chunk(zh, y, hb)]
+        for k in (1, 3, 2):
+            send("cz%d%d" % (k, hb), ref, ref, to_zh(k))
+        y_chunk_send(0, hb)
 
     outs = []
 
@@ -378,55 +417,50 @@
             hit = lax.shift_right_logical(row, 8) == want
             reb[:, place] = jnp.where(jnp.broadcast_to(hit, (128, 256)), got, reb[:, place])
 
-    def y_chunk_send(q, a):
-        ref = cent.at[chunk(a, y)]
-        send("ca%d" % q, ref, ref, to_y(1))
-        send("cb%d" % q, ref, ref, to_y(3))
-
-    def y_chunk_forward(q, a):
-        recv("ca%d" % q, cent.at[chunk(a, ym)])
-        ref = cent.at[half_chunk(a, ym, 0)]
-        send("cc%d" % q, ref, ref, to_y(1))
-        recv("cb%d" % q, cent.at[chunk(a, yp)])
-        ref = cent.at[half_chunk(a, yp, 1)]
-        send("cd%d" % q, ref, ref, to_y(3))
-
     reb[...] = jnp.zeros_like(reb)
-    zs_of = [zh] + [lax.rem(zh + 4 - q, 4) for q in (1, 2, 3)]
-    for k in (2, 1, 3):
-        ref = cent.at[own_rows]
-        send("cz%d" % k, ref, ref, to_zh(k))
-    y_chunk_send(0, zh)
+    vrecv("wm0", down_z, 0, core)
+    vsend("w20", down_z, 0, core, to_xp)
+    vsend("d_wm0", down_z, 0, core, to_core)
+    vrecv("wp0", up_z, 0, core)
+    vsend("d_wp0", up_z, 0, core, to_core)
+    y_chunk_forward(0, 0)
+    z_chunk(1, 0)
+    z_chunk(3, 0)
+    y_chunk_forward(0, 1)
     rebuild(zh, y)
-    y_chunk_forward(0, zh)
-    order = (1, 3, 2)
-    before = 0
-    for q in order:
-        a = zs_of[q]
-        recv("cz%d" % q, cent.at[chunk(a, y)])
-        y_chunk_send(q, a)
-        if before:
-            y_chunk_forward(before, zs_of[before])
-        rebuild(a, y)
-        rebuild(zs_of[before], ym)
-        rebuild(zs_of[before], yp)
-        before = q
-    y_chunk_forward(before, zs_of[before])
-    for b in (ym, yp):
-        rebuild(zs_of[before], b)
-
+    z_chunk(2, 0)
+    y_chunk_forward(1, 0)
+    y_chunk_forward(3, 0)
+    rebuild(zh, ym)
+    rebuild(zh, yp)
+    vrecv("wp1", up_z, 1, core)
+    vsend("w21", up_z, 1, core, to_xm)
+    vsend("d_wp1", up_z, 1, core, to_core)
     vrecv("wm1", down_z, 1, core)
     vsend("d_wm1", down_z, 1, core, to_core)
-    vrecv("wp0", up_z, 0, core)
-    vsend("d_wp0", up_z, 0, core, to_core)
+    z_chunk(1, 1)
+    z_chunk(3, 1)
+    y_chunk_forward(2, 0)
+    z_chunk(2, 1)
+    rebuild(zs_of[1], y)
+    rebuild(zs_of[3], y)
+    y_chunk_forward(1, 1)
+    y_chunk_forward(3, 1)
+    rebuild(zs_of[2], y)
+    y_chunk_forward(2, 1)
+    for q in (1, 3, 2):
+        rebuild(zs_of[q], ym)
+        rebuild(zs_of[q], yp)
+
     vrecv("w20", far_z, 0, core)
     vsend("d_w20", far_z, 0, core, to_core)
     vrecv("w21", far_z, 1, core)
     vsend("d_w21", far_z, 1, core, to_core)
-    for q in (0,) + order:
+    for q in (0, 1, 3, 2):
         a = zs_of[q]
-        recv("cc%d" % q, cent.at[half_chunk(a, y2, 0)])
-        recv("cd%d" % q, cent.at[half_chunk(a, y2, 1)])
+        for hb in range(2):
+            recv("cc%d%d" % (q, hb), cent.at[quarter_chunk(a, y2, hb, 0)])
+            recv("cd%d%d" % (q, hb), cent.at[quarter_chunk(a, y2, hb, 1)])
         rebuild(a, y2)
     for h in range(2):
         vrecv("d_w%d" % h, here_z, h, co)
@@ -436,26 +470,28 @@
 
     rebb[...] = reb[...].astype(BF16)
 
-    def cross_half(p):
-        def body(i, carry):
-            place = pl.ds(pl.multiple_of(i * 512 + p * 256, 256), 256)
-            part = jnp.dot(rebb[...], vg[:, place], preferred_element_type=F32)
-            xf[2 * p, i] = part[:, :128]
-            xf[2 * p + 1, i] = part[:, 128:]
-            return carry
-
-        lax.fori_loop(0, 4, body, 0)
-
-    def cross_send(k):
-        xs[k - 1] = xf[lax.rem(y + k, 4)].astype(BF16)
-        send("xa%d" % k, xs.at[k - 1], xr.at[k - 1], to_y(k))
-
-    near = lax.div(y, 2)
-    cross_half(1 - near)
-    cross_send(2)
-    cross_half(near)
-    cross_send(1)
-    cross_send(3)
+    pairs = ((2, 1), (3, 0))
+
+    def cross_part(k, p):
+        to = lax.rem(y + k, 4)
+        blocks = []
+        for z in pairs[p]:
+            column = (lax.rem(zh + z, 4) * 4 + to) * 128
+            blocks.append(vg[:, pl.ds(pl.multiple_of(column, 128), 128)])
+        got = jnp.dot(rebb[...], jnp.concatenate(blocks, axis=1), preferred_element_type=F32)
+        if k == 0:
+            xf[p, 0] = got[:, :128]
+            xf[p, 1] = got[:, 128:]
+        else:
+            xs[k - 1, p, 0] = got[:, :128].astype(BF16)
+            xs[k - 1, p, 1] = got[:, 128:].astype(BF16)
+            send("xa%d%d" % (k, p), xs.at[k - 1, p], xr.at[k - 1, p], to_y(k))
+
+    for p in range(2):
+        for k in (2, 1, 3):
+            cross_part(k, p)
+    for p in range(2):
+        cross_part(0, p)
 
     gap = rott[...] - reb[...]
     gap = jnp.sum(gap * gap, axis=0, keepdims=True)
@@ -465,14 +501,21 @@
         dist_ref[2 * cp:2 * cp + 1, :] = jnp.where(half_row, u0, pltpu.roll(u1, 64, 1))
         dist_ref[2 * cp + 1:2 * cp + 2, :] = jnp.where(half_row, pltpu.roll(u0, 64, 1), u1)
 
-    for k in (1, 3, 2):
-        recv("xa%d" % k, xr.at[k - 1])
-    xf[y] = xf[y] + xr[0].astype(F32) + xr[1].astype(F32) + xr[2].astype(F32)
-    for k in (2, 1, 3):
-        zs[k - 1] = xf[y, lax.rem(zh + k, 4)].astype(BF16)
+    def cross_sum(p):
+        for k in (1, 3, 2):
+            recv("xa%d%d" % (k, p), xr.at[k - 1, p])
+        return [xf[p, i] + xr[0, p, i].astype(F32) + xr[1, p, i].astype(F32) + xr[2, p, i].astype(F32) for i in range(2)]
+
+    def cross_zh(k, value):
+        zs[k - 1] = value.astype(BF16)
         send("xz%d" % k, zs.at[k - 1], zr.at[k - 1], to_zh(k))
-    out = xf[y, zh]
-    for k in (1, 3, 2):
+
+    two, one = cross_sum(0)
+    cross_zh(2, two)
+    cross_zh(1, one)
+    three, out = cross_sum(1)
+    cross_zh(3, three)
+    for k in (1, 2, 3):
         recv("xz%d" % k, zr.at[k - 1])
         out = out + zr[k - 1].astype(F32)
     cross_ref[...] = out.T
@@ -516,9 +559,9 @@
             pltpu.VMEM((K, DS), BF16),
             pltpu.VMEM((DS, GROUP), F32),
             pltpu.VMEM((DS, GROUP), BF16),
-            pltpu.VMEM((4, 4, DS, 128), F32),
-            pltpu.VMEM((3, 4, DS, 128), BF16),
-            pltpu.VMEM((3, 4, DS, 128), BF16),
+            pltpu.VMEM((2, 2, DS, 128), F32),
+            pltpu.VMEM((3, 2, 2, DS, 128), BF16),
+            pltpu.VMEM((3, 2, 2, DS, 128), BF16),
             pltpu.VMEM((3, DS, 128), BF16),
             pltpu.VMEM((3, DS, 128), BF16),
             pltpu.SemaphoreType.DMA((SEMS,)),

time: 95.4 us -> 89.7 us (0.940)
  the two profiles are of different devices: /device:TPU:1 before, /device:TPU:2 now
where the time goes in v3:
time: 89.7 us; the launch traced here: 88.5 us
  Pallas kernels  85.6 us (95%)
  local copies, waits for them, and re-layouts  2.2 us (2%)
    pallas_call x1, Pallas kernels, per_device(): pl.pallas_call(kernel, out_shape=(jax.ShapeDtypeStruct((K, DS), BF16), ja...  85.6 us
    unnamed x3, local copies, waits for them, and re-layouts  2.2 us

profile of v3, /device:TPU:2, one launch (start us, length us, event | category | flops | bytes accessed | tf_op | source)
XLA Modules:
  0.0 88.5 jit_solution(12145495496361022563)
XLA Ops:
  0.6 85.6 %opq_step.1 = (bf16[4096,128]{1,0:T(8,128)(2,1)S(1)}, f32[16,128]{1,0:T(8,128)S(1)}, f32[128,128]{1,0:T(8,128)S(1)}) custom-call(bf16[128,2048]{1,0:T(8,128)(2,1)} %v_ref.1, bf16[2048,128]{1,0:T(8,128)(2,1)} %r_ref.1, bf16[4096,128]{1,0:T(8,128)(2,1)} %bitcast.6, s32[16,128]{1,0:T(8,128)} %bitcast.7), custom_call_target="tpu_custom_call" | custom-call | tf_op jit(solution)/shard_map/opq_step/pallas_call | solution.py:533
  86.3 1.0 %copy.10 = bf16[1,4096,128]{2,1,0:T(8,128)(2,1)} copy(bf16[1,4096,128]{2,1,0:T(8,128)(2,1)S(1)} %bitcast.4) | data formatting | bytes 2097152
  87.2 0.6 copy.11
  87.8 0.6 copy.12

commit v4 on v3

--- a/solution.py
+++ b/solution.py
@@ -238,6 +238,7 @@
     rot_both(unit(up, 0))
     y_send("C", unit(up, 0), False)
     z_send("C", unit(up, 0))
+    vsend("w0", here, 0, core, to_z)
     y_forward("A", here * 256, 256)
     lax.fori_loop(0, 4, hi_table, 0)
 
@@ -307,8 +308,11 @@
     rot_both(unit(far, 1))
     z_send("G", unit(far, 1))
     y_send("G", unit(far, 1), True)
-    vsend("w0", here, 0, core, to_z)
     vsend("w1", here, 1, core, to_z)
+    vrecv("w0", here_z, 0, core)
+    vsend("wm0", here_z, 0, core, to_xp)
+    vsend("wp0", here_z, 0, core, to_xm)
+    vsend("d_w0", here_z, 0, core, to_core)
     z_recv("F", unit(far_z, 0))
     y_send("Fz", unit(far_z, 0), True)
     y_forward("Dz", down_z * 256 + 128, 128)
@@ -329,10 +333,15 @@
     y_last("Cz", up_z * 256, 128, False)
     y_last("Ez", up_z * 256 + 128, 128, False)
     accumulate(up_z)
-    vrecv("w0", here_z, 0, core)
-    vsend("wm0", here_z, 0, core, to_xp)
-    vsend("wp0", here_z, 0, core, to_xm)
-    vsend("d_w0", here_z, 0, core, to_core)
+    vrecv("w1", here_z, 1, core)
+    vsend("wp1", here_z, 1, core, to_xm)
+    vsend("wm1", here_z, 1, core, to_xp)
+    vsend("d_w1", here_z, 1, core, to_core)
+    vrecv("wm0", down_z, 0, core)
+    vsend("w20", down_z, 0, core, to_xp)
+    vsend("d_wm0", down_z, 0, core, to_core)
+    vrecv("wp0", up_z, 0, core)
+    vsend("d_wp0", up_z, 0, core, to_core)
     y_last("F", far * 256, 128, True)
     y_last("G", far * 256 + 128, 128, True)
     accumulate(far)
@@ -354,10 +363,11 @@
     mine = counts[4, pl.ds(hi_own, 1), :]
     cnt[...] = jnp.broadcast_to(mine, (128, 256)).T
     rott[...] = rot[y].astype(F32).T
-    vrecv("w1", here_z, 1, core)
-    vsend("wp1", here_z, 1, core, to_xm)
-    vsend("wm1", here_z, 1, core, to_xp)
-    vsend("d_w1", here_z, 1, core, to_core)
+    vrecv("wp1", up_z, 1, core)
+    vsend("w21", up_z, 1, core, to_xm)
+    vsend("d_wp1", up_z, 1, core, to_core)
+    vrecv("wm1", down_z, 1, core)
+    vsend("d_wm1", down_z, 1, core, to_core)
 
     def chunk(a, b):
         return pl.ds(pl.multiple_of(b * 1024 + a * OWN, OWN), OWN)
@@ -418,11 +428,6 @@
             reb[:, place] = jnp.where(jnp.broadcast_to(hit, (128, 256)), got, reb[:, place])
 
     reb[...] = jnp.zeros_like(reb)
-    vrecv("wm0", down_z, 0, core)
-    vsend("w20", down_z, 0, core, to_xp)
-    vsend("d_wm0", down_z, 0, core, to_core)
-    vrecv("wp0", up_z, 0, core)
-    vsend("d_wp0", up_z, 0, core, to_core)
     y_chunk_forward(0, 0)
     z_chunk(1, 0)
     z_chunk(3, 0)
@@ -433,11 +438,6 @@
     y_chunk_forward(3, 0)
     rebuild(zh, ym)
     rebuild(zh, yp)
-    vrecv("wp1", up_z, 1, core)
-    vsend("w21", up_z, 1, core, to_xm)
-    vsend("d_wp1", up_z, 1, core, to_core)
-    vrecv("wm1", down_z, 1, core)
-    vsend("d_wm1", down_z, 1, core, to_core)
     z_chunk(1, 1)
     z_chunk(3, 1)
     y_chunk_forward(2, 0)

time: 89.7 us -> 88.4 us (0.986)
  Pallas kernels: 85.6 us -> 84.7 us
    pallas_call x1, Pallas kernels: 85.6 us -> 84.7 us  [per_device(): pl.pallas_call(kernel, out_shape=(jax.ShapeDtypeStruct((K, DS), BF16), ja...]
where the time goes in v4:
time: 88.4 us; the launch traced here: 87.5 us
  Pallas kernels  84.7 us (96%)
  local copies, waits for them, and re-layouts  2.2 us (2%)
    pallas_call x1, Pallas kernels, per_device(): pl.pallas_call(kernel, out_shape=(jax.ShapeDtypeStruct((K, DS), BF16), ja...  84.7 us
    unnamed x3, local copies, waits for them, and re-layouts  2.2 us

profile of v4, /device:TPU:2, one launch (start us, length us, event | category | flops | bytes accessed | tf_op | source)
XLA Modules:
  0.0 87.5 jit_solution(1187163787506514026)
XLA Ops:
  0.6 84.7 %opq_step.1 = (bf16[4096,128]{1,0:T(8,128)(2,1)S(1)}, f32[16,128]{1,0:T(8,128)S(1)}, f32[128,128]{1,0:T(8,128)S(1)}) custom-call(bf16[128,2048]{1,0:T(8,128)(2,1)} %v_ref.1, bf16[2048,128]{1,0:T(8,128)(2,1)} %r_ref.1, bf16[4096,128]{1,0:T(8,128)(2,1)} %bitcast.6, s32[16,128]{1,0:T(8,128)} %bitcast.7), custom_call_target="tpu_custom_call" | custom-call | tf_op jit(solution)/shard_map/opq_step/pallas_call | solution.py:533
  85.3 1.0 %copy.10 = bf16[1,4096,128]{2,1,0:T(8,128)(2,1)} copy(bf16[1,4096,128]{2,1,0:T(8,128)(2,1)S(1)} %bitcast.4) | data formatting | bytes 2097152
  86.3 0.6 copy.11
  86.9 0.6 copy.12

commit v5 on v4

--- a/solution.py
+++ b/solution.py
@@ -442,6 +442,10 @@
     z_chunk(3, 1)
     y_chunk_forward(2, 0)
     z_chunk(2, 1)
+    vrecv("w20", far_z, 0, core)
+    vsend("d_w20", far_z, 0, core, to_core)
+    vrecv("w21", far_z, 1, core)
+    vsend("d_w21", far_z, 1, core, to_core)
     rebuild(zs_of[1], y)
     rebuild(zs_of[3], y)
     y_chunk_forward(1, 1)
@@ -452,10 +456,6 @@
         rebuild(zs_of[q], ym)
         rebuild(zs_of[q], yp)
 
-    vrecv("w20", far_z, 0, core)
-    vsend("d_w20", far_z, 0, core, to_core)
-    vrecv("w21", far_z, 1, core)
-    vsend("d_w21", far_z, 1, core, to_core)
     for q in (0, 1, 3, 2):
         a = zs_of[q]
         for hb in range(2):
@@ -524,6 +524,17 @@
         copy.wait()
     for copy in pending:
         copy.wait_send()
+
+
+def hand_out(a_ref, b_ref, c_ref, a_out, b_out, c_out, sem):
+    copies = [
+        pltpu.make_async_copy(src, dst, sem.at[i])
+        for i, (src, dst) in enumerate(((a_ref, a_out), (b_ref, b_out), (c_ref, c_out)))
+    ]
+    for copy in copies:
+        copy.start()
+    for copy in copies:
+        copy.wait()
 
 
 def per_device(vectors, rotation, codebook, codes):
@@ -573,6 +584,16 @@
         ),
         name="opq_step",
     )(*(pltpu.with_memory_space_constraint(t, pltpu.HBM) for t in operands))
+    whole = pl.BlockSpec(memory_space=pl.ANY)
+    cent, dist, cross = pl.pallas_call(
+        hand_out,
+        out_shape=tuple(jax.ShapeDtypeStruct(t.shape, t.dtype) for t in (cent, dist, cross)),
+        in_specs=[whole] * 3,
+        out_specs=(whole,) * 3,
+        scratch_shapes=[pltpu.SemaphoreType.DMA((3,))],
+        compiler_params=pltpu.CompilerParams(vmem_limit_bytes=4 * 1024 * 1024),
+        name="hand_out",
+    )(cent, dist, cross)
     return cent.reshape(1, K, DS), dist.reshape(GROUP, 1), cross
 
 

time: 88.4 us -> 85.8 us (0.971)
  local copies, waits for them, and re-layouts: 2.2 us -> 0 us
    unnamed x3 -> x0, local copies, waits for them, and re-layouts: 2.2 us -> none
    pallas_call x0 -> x1, Pallas kernels: none -> 1.01 us  [per_device(): pl.pallas_call(hand_out, out_shape=tuple((jax.ShapeDtypeStruct(t.shape, t...]
where the time goes in v5:
time: 85.8 us; the launch traced here: 85.7 us
  Pallas kernels  84.9 us (99%)
    pallas_call x1, Pallas kernels, per_device(): pl.pallas_call(kernel, out_shape=(jax.ShapeDtypeStruct((K, DS), BF16), ja...  83.9 us

profile of v5, /device:TPU:2, one launch (start us, length us, event | category | flops | bytes accessed | tf_op | source)
XLA Modules:
  0.0 85.7 jit_solution(13170381218307332717)
XLA Ops:
  0.6 83.9 %opq_step.1 = (bf16[4096,128]{1,0:T(8,128)(2,1)S(1)}, f32[16,128]{1,0:T(8,128)S(1)}, f32[128,128]{1,0:T(8,128)S(1)}) custom-call(bf16[128,2048]{1,0:T(8,128)(2,1)} %v_ref.1, bf16[2048,128]{1,0:T(8,128)(2,1)} %r_ref.1, bf16[4096,128]{1,0:T(8,128)(2,1)} %bitcast.4, s32[16,128]{1,0:T(8,128)} %bitcast.5), custom_call_target="tpu_custom_call" | custom-call | tf_op jit(solution)/shard_map/opq_step/pallas_call | solution.py:544
  84.5 1.0 %hand_out.1 = (bf16[4096,128]{1,0:T(8,128)(2,1)}, f32[16,128]{1,0:T(8,128)}, f32[128,128]{1,0:T(8,128)}) custom-call(bf16[4096,128]{1,0:T(8,128)(2,1)S(1)} %get-tuple-element.9.a_ref, f32[16,128]{1,0:T(8,128)S(1)} %get-tuple-element.10.b_ref, f32[128,128]{1,0:T(8,128)S(1)} %get-tuple-element.11.c_ref), custom_call_target="tpu_custom_call" | custom-call | tf_op jit(solution)/shard_map/hand_out/pallas_call | solution.py:588

commit v6 on v5

--- a/solution.py
+++ b/solution.py
@@ -333,6 +333,21 @@
     y_last("Cz", up_z * 256, 128, False)
     y_last("Ez", up_z * 256 + 128, 128, False)
     accumulate(up_z)
+    y_last("F", far * 256, 128, True)
+    y_last("G", far * 256 + 128, 128, True)
+    accumulate(far)
+    y_last("Fz", far_z * 256, 128, True)
+    y_last("Gz", far_z * 256 + 128, 128, True)
+    accumulate(far_z)
+
+    def part(hb):
+        return pl.ds(hb * 128, 128)
+
+    for hb in range(2):
+        for k in (2, 1, 3):
+            theirs = pl.ds(pl.multiple_of(lax.rem(zh + k, 4) * DS, DS), DS)
+            tsend[k - 1, part(hb), :] = tacc[part(hb), theirs].astype(BF16)
+            send("t%d%d" % (k, hb), tsend.at[k - 1, part(hb)], trecv.at[k - 1, part(hb)], to_zh(k))
     vrecv("w1", here_z, 1, core)
     vsend("wp1", here_z, 1, core, to_xm)
     vsend("wm1", here_z, 1, core, to_xp)
@@ -342,32 +357,12 @@
     vsend("d_wm0", down_z, 0, core, to_core)
     vrecv("wp0", up_z, 0, core)
     vsend("d_wp0", up_z, 0, core, to_core)
-    y_last("F", far * 256, 128, True)
-    y_last("G", far * 256 + 128, 128, True)
-    accumulate(far)
-    y_last("Fz", far_z * 256, 128, True)
-    y_last("Gz", far_z * 256 + 128, 128, True)
-    accumulate(far_z)
-
-    def part(hb):
-        return pl.ds(hb * 128, 128)
-
-    for hb in range(2):
-        for k in (2, 1, 3):
-            theirs = pl.ds(pl.multiple_of(lax.rem(zh + k, 4) * DS, DS), DS)
-            tsend[k - 1, part(hb), :] = tacc[part(hb), theirs].astype(BF16)
-            send("t%d%d" % (k, hb), tsend.at[k - 1, part(hb)], trecv.at[k - 1, part(hb)], to_zh(k))
     for k in (1, 3, 2):
         recv("n%d" % k, counts.at[k])
     counts[4] = counts[0] + counts[1] + counts[2] + counts[3]
     mine = counts[4, pl.ds(hi_own, 1), :]
     cnt[...] = jnp.broadcast_to(mine, (128, 256)).T
     rott[...] = rot[y].astype(F32).T
-    vrecv("wp1", up_z, 1, core)
-    vsend("w21", up_z, 1, core, to_xm)
-    vsend("d_wp1", up_z, 1, core, to_core)
-    vrecv("wm1", down_z, 1, core)
-    vsend("d_wm1", down_z, 1, core, to_core)
 
     def chunk(a, b):
         return pl.ds(pl.multiple_of(b * 1024 + a * OWN, OWN), OWN)
@@ -428,6 +423,11 @@
             reb[:, place] = jnp.where(jnp.broadcast_to(hit, (128, 256)), got, reb[:, place])
 
     reb[...] = jnp.zeros_like(reb)
+    vrecv("wp1", up_z, 1, core)
+    vsend("w21", up_z, 1, core, to_xm)
+    vsend("d_wp1", up_z, 1, core, to_core)
+    vrecv("wm1", down_z, 1, core)
+    vsend("d_wm1", down_z, 1, core, to_core)
     y_chunk_forward(0, 0)
     z_chunk(1, 0)
     z_chunk(3, 0)

time: 85.8 us -> 83.5 us (0.973); the launches traced: 85.7 us -> 82.2 us
  Pallas kernels: 84.9 us -> 81.4 us
    pallas_call x1, Pallas kernels: 83.9 us -> 80.4 us  [per_device(): pl.pallas_call(kernel, out_shape=(jax.ShapeDtypeStruct((K, DS), BF16), ja...]
where the time goes in v6:
time: 83.5 us; the launch traced here: 82.2 us
  Pallas kernels  81.4 us (97%)
    pallas_call x1, Pallas kernels, per_device(): pl.pallas_call(kernel, out_shape=(jax.ShapeDtypeStruct((K, DS), BF16), ja...  80.4 us

profile of v6, /device:TPU:2, one launch (start us, length us, event | category | flops | bytes accessed | tf_op | source)
XLA Modules:
  0.0 82.2 jit_solution(3294539696807919598)
XLA Ops:
  0.6 80.4 %opq_step.1 = (bf16[4096,128]{1,0:T(8,128)(2,1)S(1)}, f32[16,128]{1,0:T(8,128)S(1)}, f32[128,128]{1,0:T(8,128)S(1)}) custom-call(bf16[128,2048]{1,0:T(8,128)(2,1)} %v_ref.1, bf16[2048,128]{1,0:T(8,128)(2,1)} %r_ref.1, bf16[4096,128]{1,0:T(8,128)(2,1)} %bitcast.4, s32[16,128]{1,0:T(8,128)} %bitcast.5), custom_call_target="tpu_custom_call" | custom-call | tf_op jit(solution)/shard_map/opq_step/pallas_call | solution.py:544
  81.1 1.0 %hand_out.1 = (bf16[4096,128]{1,0:T(8,128)(2,1)}, f32[16,128]{1,0:T(8,128)}, f32[128,128]{1,0:T(8,128)}) custom-call(bf16[4096,128]{1,0:T(8,128)(2,1)S(1)} %get-tuple-element.9.a_ref, f32[16,128]{1,0:T(8,128)S(1)} %get-tuple-element.10.b_ref, f32[128,128]{1,0:T(8,128)S(1)} %get-tuple-element.11.c_ref), custom_call_target="tpu_custom_call" | custom-call | tf_op jit(solution)/shard_map/hand_out/pallas_call | solution.py:588
